TPU v7x, 256 devices: a whole 4x4x8 slice. The times are simulated.
256 devices in a mesh: pipe: 4 (over y_lo, core), ctx: 16 (over z, y_hi), tp: 4 (over x).
Axes of the slice: x: 4, y: 4 (y_hi: 2, y_lo: 2; y = y_hi * 2 + y_lo), z: 8, core: 2. Of those that a mesh axis runs over, the one named last changes fastest.
Arguments:
- segment_inputs: bfloat16 [4, 2, 2048, 4096], P('pipe', None, ('ctx', 'tp')), may hold values from -128 to 128
- keys: bfloat16 [4, 2, 2048, 512], P('pipe', None, 'ctx', 'tp'), may hold values from -64 to 64
- values: bfloat16 [4, 2, 2048, 512], P('pipe', None, 'ctx', 'tp'), may hold values from -6 to 6
- norm_gain: float32 [4, 4096], P('pipe'), may hold values from 0.1 to 1.9
- waiting_grads: bfloat16 [4, 2048, 4096], P('pipe', ('ctx', 'tp')), may hold values from -32 to 32
- output_grads: bfloat16 [1, 2048, 4096], P(None, ('ctx', 'tp')), may hold values from -32 to 32
- doc_lengths: int32 [5, 8], replicated, may hold values from 1 to 1024, as said below
Outputs:
- input_grads: bfloat16 [4, 2, 2048, 4096], P('pipe', None, ('ctx', 'tp'))
- key_grads: float32 [4, 2, 2048, 512], P('pipe', None, 'ctx', 'tp')
- value_grads: float32 [4, 2, 2048, 512], P('pipe', None, 'ctx', 'tp')
- gain_grads: float32 [4, 4096], P('pipe')
Inputs may be any that keep to these rules, and one draw needn't show every extreme that they name: `doc_lengths`: row m lists in order of position the lengths of the 8 documents packed into microbatch m's sequence; each row sums to 2048; the last document is exactly 1024 long.
All inputs are finite; a program needn't handle non-finite values.
Results may differ from a plain program's by a relative error of at most 0.009.
The roundings to bfloat16 on the way count: a program that leaves them out, or rounds other values in their place, can miss the bound.
Values may be sent and summed in bfloat16 or wider, within the bound.
A program may use at most 64 MiB of HBM per device.

v0:
```python
import jax
import jax.numpy as jnp
from jax import lax
from jax.sharding import PartitionSpec as P

HD = 128
S_DEV = 128
TICKS = 2
epsilon = 1e-05
masked_fill = -1e30


def passed_along(value, axis, by):
    count = lax.axis_size(axis)
    return lax.ppermute(value, axis, [(i, (i + by) % count) for i in range(count)])


def from_behind(value, axis, steps):
    count = lax.axis_size(axis)
    first, last = (max(0, -steps), min(count, count - steps))
    return lax.ppermute(value, axis, [(source, source + steps) for source in range(first, last)])


def row_positions(rows, half_rows, cycle_count):
    section = rows // half_rows
    offset = rows % half_rows
    owner = section // 2
    placed = jnp.where(section % 2 == 0, owner, 2 * cycle_count - 1 - owner)
    return placed * half_rows + offset


def document_starts(lengths_row, positions):
    closing = jnp.cumsum(lengths_row)
    passed = closing[None, :] <= positions[:, None]
    return jnp.sum(jnp.where(passed, lengths_row[None, :], 0), axis=1)


def keep_same(current):
    return current


def key_positions(key_first, key_count, cycle_count):
    rows = key_first + jnp.arange(key_count, dtype=jnp.int32)
    return row_positions(rows, S_DEV // 2, cycle_count)


def block_active(key_first, key_count, query_pos, query_start, cycle_count):
    key_pos = key_positions(key_first, key_count, cycle_count)
    return (jnp.min(key_pos) <= jnp.max(query_pos)) & (jnp.max(key_pos) >= jnp.min(query_start))


def score_block(query_block, key_block, query_pos, query_start, key_first, cycle_count):
    key_count = key_block.shape[0]
    key_pos = key_positions(key_first, key_count, cycle_count)
    scores = HD ** (-0.5) * jnp.einsum(
        "rkgd,skd->kgrs", query_block, key_block, preferred_element_type=jnp.float32
    )
    visible = (key_pos[None, :] <= query_pos[:, None]) & (key_pos[None, :] >= query_start[:, None])
    return (scores, visible[None, None])


def forward_update(carry, key_flat, value_flat, key_first, context):
    query_block, grad_block, query_pos, query_start, cycle_count = context
    key_count = key_flat.shape[0]

    def apply_block(current):
        row_peak, row_total, weighted = current
        key_block = key_flat.reshape(key_count, -1, HD)
        value_block = value_flat.reshape(key_count, -1, HD)
        scores, visible = score_block(
            query_block, key_block, query_pos, query_start, key_first, cycle_count
        )
        block_peak = jnp.max(jnp.where(visible, scores, masked_fill), axis=-1)
        new_peak = jnp.maximum(row_peak, block_peak)
        weights = jnp.where(visible, jnp.exp(scores - new_peak[..., None]), 0.0)
        prob_grad = jnp.einsum(
            "rkgd,skd->kgrs", grad_block, value_block, preferred_element_type=jnp.float32
        )
        return (new_peak, jnp.sum(weights, axis=-1), jnp.sum(weights * prob_grad, axis=-1))

    return lax.cond(
        block_active(key_first, key_count, query_pos, query_start, cycle_count),
        apply_block,
        keep_same,
        carry,
    )


def backward_terms(key_flat, value_flat, key_first, context, row_stats):
    query_block, grad_block, query_pos, query_start, cycle_count = context
    logsum, row_term = row_stats
    key_count = key_flat.shape[0]
    key_block = key_flat.reshape(key_count, -1, HD)
    value_block = value_flat.reshape(key_count, -1, HD)
    scale_factor = HD ** (-0.5)
    scores, visible = score_block(
        query_block, key_block, query_pos, query_start, key_first, cycle_count
    )
    prob_weights = jnp.where(visible, jnp.exp(scores - logsum[..., None]), 0.0)
    prob_grad = jnp.einsum(
        "rkgd,skd->kgrs", grad_block, value_block, preferred_element_type=jnp.float32
    )
    dscore = (prob_weights * (prob_grad - row_term[..., None])).astype(jnp.bfloat16)
    probs_low = prob_weights.astype(jnp.bfloat16)
    query_add = scale_factor * jnp.einsum(
        "kgrs,skd->rkgd", dscore, key_block, preferred_element_type=jnp.float32
    )
    key_add = scale_factor * jnp.einsum(
        "kgrs,rkgd->skd", dscore, query_block, preferred_element_type=jnp.float32
    )
    value_add = jnp.einsum(
        "kgrs,rkgd->skd", probs_low, grad_block, preferred_element_type=jnp.float32
    )
    return (query_add, key_add.reshape(key_count, -1), value_add.reshape(key_count, -1))


def segment_tick(inputs, key_local, value_local, gain_row, arriving, lengths_row):
    widened = inputs.astype(jnp.float32)
    inverse = lax.rsqrt(jnp.mean(widened * widened, axis=-1, keepdims=True) + epsilon)
    normed = widened * inverse
    queries = (normed * gain_row[None, :]).astype(jnp.bfloat16)
    query_heads, grad_heads = (
        lax.all_to_all(queries, "tp", split_axis=1, concat_axis=0, tiled=True),
        lax.all_to_all(arriving, "tp", split_axis=1, concat_axis=0, tiled=True),
    )
    row_count = key_local.shape[0]
    kv_local = key_local.shape[1] // HD
    group_size = query_heads.shape[1] // (HD * kv_local)
    query_block = query_heads.reshape(row_count, kv_local, group_size, HD)
    grad_block = grad_heads.reshape(row_count, kv_local, group_size, HD)
    cycle_count = lax.axis_size("ctx")
    cycle_place = lax.axis_index("ctx")
    query_pos = key_positions(cycle_place * row_count, row_count, cycle_count)
    query_start = document_starts(lengths_row, query_pos)
    context = (query_block, grad_block, query_pos, query_start, cycle_count)
    empty_peak = jnp.full((kv_local, group_size, row_count), masked_fill, jnp.float32)
    zero_rows = jnp.zeros((kv_local, group_size, row_count), jnp.float32)
    initial = (empty_peak, zero_rows, zero_rows)
    row_peak, row_total, weighted = forward_update(
        initial,
        lax.all_gather(key_local, "ctx", axis=0, tiled=True),
        lax.all_gather(value_local, "ctx", axis=0, tiled=True),
        jnp.int32(0),
        context,
    )
    row_stats = (row_peak + jnp.log(row_total), weighted / row_total)
    query_zero = jnp.zeros((row_count, kv_local, group_size, HD), jnp.float32)

    def cycle_turn(cycle_step, carry):
        key_block, value_block, key_grad, value_grad, query_grad = carry
        owner_index = (cycle_place - cycle_step) % cycle_count
        block_first = owner_index * row_count

        def apply_terms(current):
            added_terms = backward_terms(key_block, value_block, block_first, context, row_stats)
            return (
                current[0] + added_terms[1],
                current[1] + added_terms[2],
                current[2] + added_terms[0],
            )

        key_grad, value_grad, query_grad = lax.cond(
            block_active(block_first, row_count, query_pos, query_start, cycle_count),
            apply_terms,
            keep_same,
            (key_grad, value_grad, query_grad),
        )
        key_block, value_block = passed_along((key_block, value_block), "ctx", 1)
        key_grad, value_grad = passed_along((key_grad, value_grad), "ctx", 1)
        return (key_block, value_block, key_grad, value_grad, query_grad)

    zero_kv = jnp.zeros(key_local.shape, jnp.float32)
    finished = lax.fori_loop(
        0, cycle_count, cycle_turn, (key_local, value_local, zero_kv, zero_kv, query_zero)
    )
    key_grad, value_grad, query_grad = (finished[2], finished[3], finished[4])
    query_low = query_grad.reshape(row_count, -1).astype(jnp.bfloat16)
    grad_rows = lax.all_to_all(query_low, "tp", split_axis=0, concat_axis=1, tiled=True)
    rounded = grad_rows.astype(jnp.float32)
    scaled = rounded * gain_row[None, :]
    coupling = jnp.mean(scaled * normed, axis=-1, keepdims=True)
    input_grad = (arriving.astype(jnp.float32) + inverse * (scaled - normed * coupling)).astype(
        jnp.bfloat16
    )
    gain_part = jnp.sum(rounded * normed, axis=0)
    return (input_grad, key_grad, value_grad, gain_part)


def on_device(segment_inputs, keys, values, norm_gain, waiting_grads, output_grads, doc_lengths):
    segment_index = lax.axis_index("pipe")
    last_segment = lax.axis_size("pipe") - 1
    gain_row = norm_gain[0]
    arriving = waiting_grads[0]
    input_list = []
    key_list = []
    value_list = []
    gain_running = jnp.zeros(gain_row.shape, jnp.float32)
    for tick_index in range(TICKS):
        micro_index = segment_index + tick_index
        lengths_row = lax.dynamic_index_in_dim(doc_lengths, micro_index, 0, keepdims=False)
        input_grad, key_grad, value_grad, gain_part = segment_tick(
            segment_inputs[0, tick_index],
            keys[0, tick_index],
            values[0, tick_index],
            gain_row,
            arriving,
            lengths_row,
        )
        input_list.append(input_grad)
        key_list.append(key_grad)
        value_list.append(value_grad)
        gain_running = gain_running + gain_part
        if tick_index + 1 < TICKS:
            arrived = from_behind(input_grad, "pipe", -1)
            arriving = jnp.where(segment_index == last_segment, output_grads[tick_index], arrived)
    gain_grads = lax.psum(gain_running, ("ctx", "tp"))
    return (
        jnp.stack(input_list)[None],
        jnp.stack(key_list)[None],
        jnp.stack(value_list)[None],
        gain_grads[None],
    )


def solution(mesh):
    in_specs = (
        P("pipe", None, ("ctx", "tp"), None),
        P("pipe", None, "ctx", "tp"),
        P("pipe", None, "ctx", "tp"),
        P("pipe", None),
        P("pipe", ("ctx", "tp"), None),
        P(None, ("ctx", "tp"), None),
        P(),
    )
    out_specs = (
        P("pipe", None, ("ctx", "tp"), None),
        P("pipe", None, "ctx", "tp"),
        P("pipe", None, "ctx", "tp"),
        P("pipe", None),
    )
    return jax.shard_map(
        on_device, mesh=mesh, in_specs=in_specs, out_specs=out_specs, check_vma=False
    )
```

profile of v0, /device:TPU:8, one launch (start us, length us, event | category | flops | bytes accessed | tf_op | source)
XLA Modules:
  0.0 1165.9 jit_solution(12238675916187327474)
XLA Ops:
  6.3 4.3 all-to-all-start
  21.4 46.2 %all-gather = bf16[1,1,2048,128]{3,2,1,0:T(8,128)(2,1)S(1)} all-gather(bf16[1,1,128,128]{3,2,1,0:T(8,128)(2,1)S(1)} %get-tuple-element.1508), channel_id=2, replica_groups=mesh['pipe'=4,'ctx'=16,'tp'=4] {'ctx'}, dimensions={2}, use_global_device_ids=true | all-gather | bytes 557056 | tf_op jit(solution)/shard_map/all_gather | solution.py:141
  67.7 4.5 all-to-all-start.1
  72.2 40.6 %all-gather.1 = bf16[1,1,2048,128]{3,2,1,0:T(8,128)(2,1)} all-gather(bf16[1,1,128,128]{3,2,1,0:T(8,128)(2,1)S(1)} %get-tuple-element.1495), channel_id=3, replica_groups=mesh['pipe'=4,'ctx'=16,'tp'=4] {'ctx'}, dimensions={2}, use_global_device_ids=true | all-gather | bytes 557056 | tf_op jit(solution)/shard_map/all_gather | solution.py:142
  113.0 6.8 conditional.4
  120.0 273.9 %while.50 = (s32[]{:T(128)}, bf16[128,128]{1,0:T(8,128)(2,1)S(1)}, bf16[128,128]{1,0:T(8,128)(2,1)S(1)}, f32[128,128]{1,0:T(8,128)S(1)}, f32[128,128]{1,0:T(8,12...) while((s32[]{:T(128)}, bf16[128,128]{1,0:T(8,128)(2,1)S(1)}, ...), condition=%wide.region_17.18_spmd.clone, body=%wide.region_12.17_spmd.clone.sunk | while | flops 169071120 | bytes 6050608 | solution.py:173
  124.7 3.7 collective-permute-start.2
  133.1 3.2 collective-permute-done.3
  145.4 4.3 collective-permute-start.1
  159.8 3.5 collective-permute-start.3
  167.7 3.1 collective-permute-done
  182.6 3.1 collective-permute-done.2
  192.8 3.3 collective-permute-start.3
  198.5 3.0 collective-permute-start.1
  211.9 4.9 collective-permute-start.3
  219.8 4.8 collective-permute-done
  233.5 4.1 collective-permute-done.2
  245.1 3.3 collective-permute-start.3
  249.4 4.5 collective-permute-start.1
  264.2 2.7 collective-permute-start.3
  282.3 4.7 collective-permute-start.1
  297.2 2.9 collective-permute-start.3
  302.6 2.8 collective-permute-start.1
  315.6 2.8 collective-permute-start.3
  334.3 3.1 collective-permute-start.1
  347.7 4.5 collective-permute-start.3
  352.7 2.8 collective-permute-start.1
  355.6 4.1 collective-permute-done
  381.0 4.3 collective-permute-start.3
  386.3 4.7 collective-permute-start.1
  394.9 5.4 all-to-all-start.2
  400.3 6.7 all-to-all-done.2
  411.5 41.4 %all-gather.2 = bf16[1,1,2048,128]{3,2,1,0:T(8,128)(2,1)S(1)} all-gather(bf16[1,1,128,128]{3,2,1,0:T(8,128)(2,1)S(1)} %get-tuple-element.1505), channel_id=4, replica_groups=mesh['pipe'=4,'ctx'=16,'tp'=4] {'ctx'}, dimensions={2}, use_global_device_ids=true | all-gather | bytes 557056 | tf_op jit(solution)/shard_map/all_gather | solution.py:141
  454.9 41.8 %all-gather.3 = bf16[1,1,2048,128]{3,2,1,0:T(8,128)(2,1)} all-gather(bf16[1,1,128,128]{3,2,1,0:T(8,128)(2,1)S(1)} %get-tuple-element.1492), channel_id=5, replica_groups=mesh['pipe'=4,'ctx'=16,'tp'=4] {'ctx'}, dimensions={2}, use_global_device_ids=true | all-gather | bytes 557056 | tf_op jit(solution)/shard_map/all_gather | solution.py:142
  496.7 3.4 all-to-all-start.3
  502.7 4.1 all-to-all-done.3
  506.8 4.0 all-to-all-start.4
  512.4 5.1 all-to-all-done.4
  518.6 6.9 conditional.5
  525.6 273.6 %while.51 = (s32[]{:T(128)}, bf16[128,128]{1,0:T(8,128)(2,1)S(1)}, bf16[128,128]{1,0:T(8,128)(2,1)S(1)}, f32[128,128]{1,0:T(8,128)S(1)}, f32[128,128]{1,0:T(8,12...) while((s32[]{:T(128)}, bf16[128,128]{1,0:T(8,128)(2,1)S(1)}, ...), condition=%wide.region_33.34_spmd.clone, body=%wide.region_28.33_spmd.clone.sunk | while | flops 169071120 | bytes 6050608 | solution.py:173
  535.4 3.6 collective-permute-done.6
  550.4 4.7 collective-permute-start.5
  562.7 2.7 collective-permute-start.6
  567.5 3.6 collective-permute-start.4
  575.0 3.6 collective-permute-done.5
  587.4 3.9 collective-permute-done.6
  603.3 3.1 collective-permute-start.5
  616.8 4.9 collective-permute-start.7
  624.7 4.5 collective-permute-done.4
  638.8 3.5 collective-permute-done.6
  650.0 4.1 collective-permute-start.7
  655.0 4.7 collective-permute-start.5
  667.4 2.7 collective-permute-start.6
  670.0 2.6 collective-permute-start.7
  688.3 3.7 collective-permute-start.5
  702.3 3.1 collective-permute-start.7
  740.2 3.1 collective-permute-start.5
  753.7 4.9 collective-permute-start.7
  761.6 4.5 collective-permute-done.4
  786.8 3.7 collective-permute-start.7
  791.7 4.7 collective-permute-start.5
  800.3 3.4 all-to-all-start.5
  805.0 5.3 all-to-all-done.5
  810.8 353.9 %psum.7 = f32[1,4096]{1,0:T(1,128)} all-reduce(f32[1,4096]{1,0:T(1,128)S(1)} %bitcast.426), channel_id=1, replica_groups=mesh['pipe'=4,'ctx'=16,'tp'=4] {'ctx','tp'}, use_global_device_ids=true, to_apply=%region_37.38 | all-reduce | flops 4096 | bytes 32768 | tf_op jit(solution)/shard_map/psum | solution.py:216
  (956 shorter events, 382.2 us)
Async XLA Ops:
  6.3 61.3 %all-to-all-start = ((bf16[32,4,1024]{2,0,1:T(8,128)(2,1)}), bf16[32,4,1024]{2,0,1:T(8,128)(2,1)S(1)}, u32[]{:S(2)}, u32[]{:S(2)}) async-start(bf16[32,4,1024]{2,0,1:T(8,128)(2,1)} %multiply_convert_fusion.1), calls=%async_computation | async-start | bytes 524288 | tf_op jit(solution)/shard_map/all_to_all | solution.py:123
  67.7 45.2 %all-to-all-start.1 = ((bf16[32,4,1024]{2,0,1:T(8,128)(2,1)}), bf16[32,4,1024]{2,0,1:T(8,128)(2,1)S(1)}, u32[]{:S(2)}, u32[]{:S(2)}) async-start(bf16[32,4,1024]{2,0,1:T(8,128)(2,1)} %copy.84), calls=%async_computation.1 | async-start | bytes 524288 | tf_op jit(solution)/shard_map/all_to_all | solution.py:124
  124.7 8.4 collective-permute-start.2
  128.6 8.2 collective-permute-start
  143.0 8.3 collective-permute-start.2
  143.1 9.3 collective-permute-start.3
  144.4 8.3 collective-permute-start
  157.8 9.0 collective-permute-start.2
  177.7 8.0 collective-permute-start.2
  177.8 8.6 collective-permute-start.3
  192.7 8.8 collective-permute-start.2
  192.8 8.7 collective-permute-start.3
  210.7 8.1 collective-permute-start.2
  216.8 8.1 collective-permute-start.1
  229.7 8.0 collective-permute-start.2
  229.7 8.7 collective-permute-start.3
  232.2 8.1 collective-permute-start.1
  245.0 9.0 collective-permute-start.2
  245.1 8.9 collective-permute-start.3
  261.7 8.4 collective-permute-start.2
  267.0 8.1 collective-permute-start.1
  279.8 8.6 collective-permute-start.2
  279.8 9.8 collective-permute-start.3
  281.5 8.5 collective-permute-start
  282.3 8.0 collective-permute-start.1
  295.0 10.4 collective-permute-start.2
  297.2 8.2 collective-permute-start.3
  331.1 8.6 collective-permute-start.3
  346.5 9.0 collective-permute-start.2
  380.8 10.3 collective-permute-start.2
  381.0 10.1 collective-permute-start.3
  394.9 12.0 %all-to-all-start.2 = ((bf16[4,32,1024]{2,1,0:T(8,128)(2,1)}), bf16[4,32,1024]{2,1,0:T(8,128)(2,1)S(1)}, u32[]{:S(2)}, u32[]{:S(2)}) async-start(bf16[4,32,1024]{2,1,0:T(8,128)(2,1)} %convert_element_type.172), calls=%async_computation.2 | async-start | bytes 524288 | tf_op jit(solution)/shard_map/all_to_all | solution.py:178
  409.6 91.3 %collective-permute-start.8 = (bf16[32,4096]{1,0:T(8,128)(2,1)}, bf16[32,4096]{1,0:T(8,128)(2,1)}, u32[]{:S(2)}, u32[]{:S(2)}) collective-permute-start(bf16[32,4096]{1,0:T(8,128)(2,1)} %fusion.122), channel_id=1, source_target_pairs={{64,0},{128,64},{192,128},{65,1},{129,65},{193,129},{66,2},{130,66... | collective-permute-start | bytes 786440 | tf_op jit(solution)/shard_map/ppermute | solution.py:21
  496.7 10.1 all-to-all-start.3
  506.8 10.8 all-to-all-start.4
  530.4 8.6 collective-permute-start.6
  533.1 8.1 collective-permute-start.4
  547.6 8.1 collective-permute-start.6
  547.7 8.7 collective-permute-start.7
  562.7 9.6 collective-permute-start.6
  583.4 8.6 collective-permute-start.7
  598.3 8.1 collective-permute-start.6
  598.4 8.6 collective-permute-start.7
  615.6 8.7 collective-permute-start.6
  634.6 8.5 collective-permute-start.7
  636.8 8.3 collective-permute-start.5
  649.9 9.8 collective-permute-start.6
  650.0 9.8 collective-permute-start.7
  667.4 8.1 collective-permute-start.6
  670.0 8.0 collective-permute-start.7
  685.3 8.3 collective-permute-start.6
  685.4 8.9 collective-permute-start.7
  700.6 9.8 collective-permute-start.6
  702.3 8.1 collective-permute-start.7
  720.2 8.0 collective-permute-start.6
  720.6 8.2 collective-permute-start.7
  735.9 8.0 collective-permute-start.6
  736.2 8.4 collective-permute-start.7
  752.5 8.8 collective-permute-start.6
  771.2 8.0 collective-permute-start.6
  771.6 8.3 collective-permute-start.7
  786.7 9.7 collective-permute-start.6
  786.8 9.6 collective-permute-start.7
  800.3 10.1 all-to-all-start.5
  (82 other events, 3647.2 us)
where the time goes:
time: 1170 us
  blocking collectives  524 us (45%)
  starting transfers between devices  263 us (22%)
  waiting for transfers between devices  180 us (15%)
  loops' own time  85 us (7%)
  other arithmetic  51.5 us (4%)
  matrix products  46.7 us (4%)
    psum x1, blocking collectives, on_device(): gain_grads = lax.psum(gain_running, ('ctx', 'tp'))  354 us
    ppermute x128, starting transfers between devices, passed_along(): lax.ppermute(value, axis, [(i, (i + by) % count) for i in range(count)])  236 us
    ppermute x128, waiting for transfers between devices, passed_along(): lax.ppermute(value, axis, [(i, (i + by) % count) for i in range(count)])  159 us
    all_gather x2, blocking collectives, segment_tick(): lax.all_gather(key_local, 'ctx', axis=0, tiled=True)  87.6 us
    all_gather x2, blocking collectives, segment_tick(): lax.all_gather(value_local, 'ctx', axis=0, tiled=True)  82.4 us
    another operation x2, loops' own time, segment_tick(): lax.fori_loop(0, cycle_count, cycle_turn, (key_local, value_local, zero_k...  82.4 us
    reduce_max x33, other arithmetic, block_active(): jnp.max(key_pos) >= jnp.min(query_start)  23.7 us
  transfers between devices with their start and end apart: 135, of which 110 were waited for; matrix products, arithmetic and copies ran while one was open for 1% of the time, Pallas kernels for 0%

commit v1 on v0

--- a/solution.py
+++ b/solution.py
@@ -213,7 +213,9 @@
         if tick_index + 1 < TICKS:
             arrived = from_behind(input_grad, "pipe", -1)
             arriving = jnp.where(segment_index == last_segment, output_grads[tick_index], arrived)
-    gain_grads = lax.psum(gain_running, ("ctx", "tp"))
+    gain_grads = gain_running
+    for mesh_axis in ("tp", "ctx"):
+        gain_grads = lax.psum(gain_grads, mesh_axis)
     return (
         jnp.stack(input_list)[None],
         jnp.stack(key_list)[None],

time: 1170 us -> 904 us (0.77)
  blocking collectives: 524 us -> 260 us
    psum x1 -> x2, blocking collectives: 354 us -> 89.7 us  [on_device(): gain_grads = lax.psum(gain_grads, mesh_axis)]
  transfers between devices with their start and end apart: 135 -> 135, of which waited for: 110 -> 110; matrix products, arithmetic and copies ran while one was open for 1% -> 2% of each run, Pallas kernels for 0% -> 0%
where the time goes in v1:
time: 904 us; the launch traced here: 902 us
  starting transfers between devices  263 us (29%)
  blocking collectives  260 us (29%)
  waiting for transfers between devices  180 us (20%)
  loops' own time  85 us (9%)
  other arithmetic  51.5 us (6%)
  matrix products  46.7 us (5%)
  local copies, waits for them, and re-layouts  10.6 us (1%)
    ppermute x128, starting transfers between devices, passed_along(): lax.ppermute(value, axis, [(i, (i + by) % count) for i in range(count)])  236 us
    ppermute x128, waiting for transfers between devices, passed_along(): lax.ppermute(value, axis, [(i, (i + by) % count) for i in range(count)])  159 us
    psum x2, blocking collectives, on_device(): gain_grads = lax.psum(gain_grads, mesh_axis)  89.7 us
    all_gather x2, blocking collectives, segment_tick(): lax.all_gather(key_local, 'ctx', axis=0, tiled=True)  87.6 us
    all_gather x2, blocking collectives, segment_tick(): lax.all_gather(value_local, 'ctx', axis=0, tiled=True)  82.4 us
    another operation x2, loops' own time, segment_tick(): lax.fori_loop(0, cycle_count, cycle_turn, (key_local, value_local, zero_k...  82.4 us
    reduce_max x33, other arithmetic, block_active(): jnp.max(key_pos) >= jnp.min(query_start)  23.7 us
  transfers between devices with their start and end apart: 135, of which 110 were waited for; matrix products, arithmetic and copies ran while one was open for 2% of the time, Pallas kernels for 0%

profile of v1, /device:TPU:8, one launch (start us, length us, event | category | flops | bytes accessed | tf_op | source)
XLA Modules:
  0.0 901.7 jit_solution(529617668611639105)
XLA Ops:
  6.3 4.3 all-to-all-start
  21.4 46.2 %all-gather = bf16[1,1,2048,128]{3,2,1,0:T(8,128)(2,1)S(1)} all-gather(bf16[1,1,128,128]{3,2,1,0:T(8,128)(2,1)S(1)} %get-tuple-element.1508), channel_id=2, replica_groups=mesh['pipe'=4,'ctx'=16,'tp'=4] {'ctx'}, dimensions={2}, use_global_device_ids=true | all-gather | bytes 557056 | tf_op jit(solution)/shard_map/all_gather | solution.py:141
  67.7 4.5 all-to-all-start.1
  72.2 40.6 %all-gather.1 = bf16[1,1,2048,128]{3,2,1,0:T(8,128)(2,1)} all-gather(bf16[1,1,128,128]{3,2,1,0:T(8,128)(2,1)S(1)} %get-tuple-element.1495), channel_id=3, replica_groups=mesh['pipe'=4,'ctx'=16,'tp'=4] {'ctx'}, dimensions={2}, use_global_device_ids=true | all-gather | bytes 557056 | tf_op jit(solution)/shard_map/all_gather | solution.py:142
  113.0 6.8 conditional.4
  120.0 273.9 %while.50 = (s32[]{:T(128)}, bf16[128,128]{1,0:T(8,128)(2,1)S(1)}, bf16[128,128]{1,0:T(8,128)(2,1)S(1)}, f32[128,128]{1,0:T(8,128)S(1)}, f32[128,128]{1,0:T(8,12...) while((s32[]{:T(128)}, bf16[128,128]{1,0:T(8,128)(2,1)S(1)}, ...), condition=%wide.region_17.18_spmd.clone, body=%wide.region_12.17_spmd.clone.sunk | while | flops 169071120 | bytes 6050608 | solution.py:173
  124.7 3.7 collective-permute-start.2
  133.1 3.2 collective-permute-done.3
  145.4 4.3 collective-permute-start.1
  159.8 3.5 collective-permute-start.3
  167.7 3.1 collective-permute-done
  182.6 3.1 collective-permute-done.2
  192.8 3.3 collective-permute-start.3
  198.5 3.0 collective-permute-start.1
  211.9 4.9 collective-permute-start.3
  219.8 4.8 collective-permute-done
  233.5 4.1 collective-permute-done.2
  245.1 3.3 collective-permute-start.3
  249.4 4.5 collective-permute-start.1
  264.2 2.7 collective-permute-start.3
  282.3 4.7 collective-permute-start.1
  297.2 2.9 collective-permute-start.3
  302.6 2.8 collective-permute-start.1
  315.6 2.8 collective-permute-start.3
  334.3 3.1 collective-permute-start.1
  347.7 4.5 collective-permute-start.3
  352.7 2.8 collective-permute-start.1
  355.6 4.1 collective-permute-done
  381.0 4.3 collective-permute-start.3
  386.3 4.7 collective-permute-start.1
  394.9 5.4 all-to-all-start.2
  400.3 6.7 all-to-all-done.2
  411.5 41.4 %all-gather.2 = bf16[1,1,2048,128]{3,2,1,0:T(8,128)(2,1)S(1)} all-gather(bf16[1,1,128,128]{3,2,1,0:T(8,128)(2,1)S(1)} %get-tuple-element.1505), channel_id=4, replica_groups=mesh['pipe'=4,'ctx'=16,'tp'=4] {'ctx'}, dimensions={2}, use_global_device_ids=true | all-gather | bytes 557056 | tf_op jit(solution)/shard_map/all_gather | solution.py:141
  454.9 41.8 %all-gather.3 = bf16[1,1,2048,128]{3,2,1,0:T(8,128)(2,1)} all-gather(bf16[1,1,128,128]{3,2,1,0:T(8,128)(2,1)S(1)} %get-tuple-element.1492), channel_id=5, replica_groups=mesh['pipe'=4,'ctx'=16,'tp'=4] {'ctx'}, dimensions={2}, use_global_device_ids=true | all-gather | bytes 557056 | tf_op jit(solution)/shard_map/all_gather | solution.py:142
  496.7 3.4 all-to-all-start.3
  502.7 4.1 all-to-all-done.3
  506.8 4.0 all-to-all-start.4
  512.4 5.1 all-to-all-done.4
  518.6 6.9 conditional.5
  525.6 273.6 %while.51 = (s32[]{:T(128)}, bf16[128,128]{1,0:T(8,128)(2,1)S(1)}, bf16[128,128]{1,0:T(8,128)(2,1)S(1)}, f32[128,128]{1,0:T(8,128)S(1)}, f32[128,128]{1,0:T(8,12...) while((s32[]{:T(128)}, bf16[128,128]{1,0:T(8,128)(2,1)S(1)}, ...), condition=%wide.region_33.34_spmd.clone, body=%wide.region_28.33_spmd.clone.sunk | while | flops 169071120 | bytes 6050608 | solution.py:173
  535.4 3.6 collective-permute-done.6
  550.4 4.7 collective-permute-start.5
  562.7 2.7 collective-permute-start.6
  567.5 3.6 collective-permute-start.4
  575.0 3.6 collective-permute-done.5
  587.4 3.9 collective-permute-done.6
  603.3 3.1 collective-permute-start.5
  616.8 4.9 collective-permute-start.7
  624.7 4.5 collective-permute-done.4
  638.8 3.5 collective-permute-done.6
  650.0 4.1 collective-permute-start.7
  655.0 4.7 collective-permute-start.5
  667.4 2.7 collective-permute-start.6
  688.3 3.7 collective-permute-start.5
  702.3 3.1 collective-permute-start.7
  740.2 3.1 collective-permute-start.5
  753.7 4.9 collective-permute-start.7
  761.6 4.5 collective-permute-done.4
  786.8 3.7 collective-permute-start.7
  791.7 4.7 collective-permute-start.5
  800.3 3.4 all-to-all-start.5
  805.0 5.3 all-to-all-done.5
  810.8 15.3 %psum.14 = f32[4096]{0:T(1024)S(1)} all-reduce(f32[4096]{0:T(1024)S(1)} %bitcast.428), channel_id=1, replica_groups=mesh['pipe'=4,'ctx'=16,'tp'=4] {'tp'}, use_global_device_ids=true, to_apply=%region_37.38 | all-reduce | flops 4096 | bytes 32768 | tf_op jit(solution)/shard_map/psum | solution.py:218
  826.1 74.4 %psum.15 = f32[1,4096]{1,0:T(1,128)} all-reduce(f32[1,4096]{1,0:T(1,128)S(1)} %bitcast.429), channel_id=1, replica_groups=mesh['pipe'=4,'ctx'=16,'tp'=4] {'ctx'}, use_global_device_ids=true, to_apply=%region_38.39 | all-reduce | flops 4096 | bytes 32768 | tf_op jit(solution)/shard_map/psum | solution.py:218
  (957 shorter events, 384.8 us)
Async XLA Ops:
  6.3 61.3 %all-to-all-start = ((bf16[32,4,1024]{2,0,1:T(8,128)(2,1)}), bf16[32,4,1024]{2,0,1:T(8,128)(2,1)S(1)}, u32[]{:S(2)}, u32[]{:S(2)}) async-start(bf16[32,4,1024]{2,0,1:T(8,128)(2,1)} %multiply_convert_fusion.1), calls=%async_computation | async-start | bytes 524288 | tf_op jit(solution)/shard_map/all_to_all | solution.py:123
  67.7 45.2 %all-to-all-start.1 = ((bf16[32,4,1024]{2,0,1:T(8,128)(2,1)}), bf16[32,4,1024]{2,0,1:T(8,128)(2,1)S(1)}, u32[]{:S(2)}, u32[]{:S(2)}) async-start(bf16[32,4,1024]{2,0,1:T(8,128)(2,1)} %copy.84), calls=%async_computation.1 | async-start | bytes 524288 | tf_op jit(solution)/shard_map/all_to_all | solution.py:124
  124.7 8.4 collective-permute-start.2
  128.6 8.2 collective-permute-start
  143.0 8.3 collective-permute-start.2
  143.1 9.3 %collective-permute-start.3 = (f32[128,128]{1,0:T(8,128)S(1)}, f32[128,128]{1,0:T(8,128)S(1)}, u32[]{:S(2)}, u32[]{:S(2)}) collective-permute-start(f32[128,128]{1,0:T(8,128)S(1)} %get-tuple-element.1701), channel_id=1, source_target_pairs={{0,4},{4,8},{8,12},{12,16},{16,20},{20,24},{24,28},{28,32},{32,36}... | collective-permute-start | bytes 196616 | tf_op jit(solution)/shard_map/while/body/eval_jaxpr/ppermute | solution.py:15
  144.4 8.3 collective-permute-start
  157.8 9.0 collective-permute-start.2
  177.7 8.0 collective-permute-start.2
  177.8 8.6 collective-permute-start.3
  192.7 8.8 collective-permute-start.2
  192.8 8.7 collective-permute-start.3
  210.7 8.1 collective-permute-start.2
  216.8 8.1 collective-permute-start.1
  229.7 8.0 collective-permute-start.2
  229.7 8.7 collective-permute-start.3
  232.2 8.1 collective-permute-start.1
  245.0 9.0 collective-permute-start.2
  245.1 8.9 collective-permute-start.3
  261.7 8.4 collective-permute-start.2
  267.0 8.1 collective-permute-start.1
  279.8 8.6 collective-permute-start.2
  279.8 9.8 %collective-permute-start.3 = (f32[128,128]{1,0:T(8,128)S(1)}, f32[128,128]{1,0:T(8,128)S(1)}, u32[]{:S(2)}, u32[]{:S(2)}) collective-permute-start(f32[128,128]{1,0:T(8,128)S(1)} %get-tuple-element.1701), channel_id=1, source_target_pairs={{0,4},{4,8},{8,12},{12,16},{16,20},{20,24},{24,28},{28,32},{32,36}... | collective-permute-start | bytes 196616 | tf_op jit(solution)/shard_map/while/body/eval_jaxpr/ppermute | solution.py:15
  281.5 8.5 collective-permute-start
  282.3 8.0 collective-permute-start.1
  295.0 10.4 %collective-permute-start.2 = (f32[128,128]{1,0:T(8,128)S(1)}, f32[128,128]{1,0:T(8,128)S(1)}, u32[]{:S(2)}, u32[]{:S(2)}) collective-permute-start(f32[128,128]{1,0:T(8,128)S(1)} %get-tuple-element.1700), channel_id=1, source_target_pairs={{0,4},{4,8},{8,12},{12,16},{16,20},{20,24},{24,28},{28,32},{32,36}... | collective-permute-start | bytes 196616 | tf_op jit(solution)/shard_map/while/body/eval_jaxpr/ppermute | solution.py:15
  297.2 8.2 collective-permute-start.3
  331.1 8.6 collective-permute-start.3
  346.5 9.0 collective-permute-start.2
  380.8 10.3 %collective-permute-start.2 = (f32[128,128]{1,0:T(8,128)S(1)}, f32[128,128]{1,0:T(8,128)S(1)}, u32[]{:S(2)}, u32[]{:S(2)}) collective-permute-start(f32[128,128]{1,0:T(8,128)S(1)} %get-tuple-element.1700), channel_id=1, source_target_pairs={{0,4},{4,8},{8,12},{12,16},{16,20},{20,24},{24,28},{28,32},{32,36}... | collective-permute-start | bytes 196616 | tf_op jit(solution)/shard_map/while/body/eval_jaxpr/ppermute | solution.py:15
  381.0 10.1 %collective-permute-start.3 = (f32[128,128]{1,0:T(8,128)S(1)}, f32[128,128]{1,0:T(8,128)S(1)}, u32[]{:S(2)}, u32[]{:S(2)}) collective-permute-start(f32[128,128]{1,0:T(8,128)S(1)} %get-tuple-element.1701), channel_id=1, source_target_pairs={{0,4},{4,8},{8,12},{12,16},{16,20},{20,24},{24,28},{28,32},{32,36}... | collective-permute-start | bytes 196616 | tf_op jit(solution)/shard_map/while/body/eval_jaxpr/ppermute | solution.py:15
  394.9 12.0 %all-to-all-start.2 = ((bf16[4,32,1024]{2,1,0:T(8,128)(2,1)}), bf16[4,32,1024]{2,1,0:T(8,128)(2,1)S(1)}, u32[]{:S(2)}, u32[]{:S(2)}) async-start(bf16[4,32,1024]{2,1,0:T(8,128)(2,1)} %convert_element_type.172), calls=%async_computation.2 | async-start | bytes 524288 | tf_op jit(solution)/shard_map/all_to_all | solution.py:178
  409.6 91.3 %collective-permute-start.8 = (bf16[32,4096]{1,0:T(8,128)(2,1)}, bf16[32,4096]{1,0:T(8,128)(2,1)}, u32[]{:S(2)}, u32[]{:S(2)}) collective-permute-start(bf16[32,4096]{1,0:T(8,128)(2,1)} %fusion.122), channel_id=1, source_target_pairs={{64,0},{128,64},{192,128},{65,1},{129,65},{193,129},{66,2},{130,66... | collective-permute-start | bytes 786440 | tf_op jit(solution)/shard_map/ppermute | solution.py:21
  496.7 10.1 %all-to-all-start.3 = ((bf16[32,4,1024]{2,0,1:T(8,128)(2,1)}), bf16[32,4,1024]{2,0,1:T(8,128)(2,1)S(1)}, u32[]{:S(2)}, u32[]{:S(2)}) async-start(bf16[32,4,1024]{2,0,1:T(8,128)(2,1)} %get-tuple-element.1500), calls=%async_computation.3 | async-start | bytes 524288 | tf_op jit(solution)/shard_map/all_to_all | solution.py:123
  506.8 10.8 %all-to-all-start.4 = ((bf16[32,4,1024]{2,0,1:T(8,128)(2,1)}), bf16[32,4,1024]{2,0,1:T(8,128)(2,1)}, u32[]{:S(2)}, u32[]{:S(2)}) async-start(bf16[32,4,1024]{2,0,1:T(8,128)(2,1)} %bitcast.397), calls=%async_computation.4 | async-start | bytes 524288 | tf_op jit(solution)/shard_map/all_to_all | solution.py:124
  530.4 8.6 collective-permute-start.6
  533.1 8.1 collective-permute-start.4
  547.6 8.1 collective-permute-start.6
  547.7 8.7 collective-permute-start.7
  562.7 9.6 %collective-permute-start.6 = (f32[128,128]{1,0:T(8,128)S(1)}, f32[128,128]{1,0:T(8,128)S(1)}, u32[]{:S(2)}, u32[]{:S(2)}) collective-permute-start(f32[128,128]{1,0:T(8,128)S(1)} %get-tuple-element.1724), channel_id=1, source_target_pairs={{0,4},{4,8},{8,12},{12,16},{16,20},{20,24},{24,28},{28,32},{32,36}... | collective-permute-start | bytes 196616 | tf_op jit(solution)/shard_map/while/body/eval_jaxpr/ppermute | solution.py:15
  583.4 8.6 collective-permute-start.7
  598.3 8.1 collective-permute-start.6
  598.4 8.6 collective-permute-start.7
  615.6 8.7 collective-permute-start.6
  634.6 8.5 collective-permute-start.7
  636.8 8.3 collective-permute-start.5
  649.9 9.8 %collective-permute-start.6 = (f32[128,128]{1,0:T(8,128)S(1)}, f32[128,128]{1,0:T(8,128)S(1)}, u32[]{:S(2)}, u32[]{:S(2)}) collective-permute-start(f32[128,128]{1,0:T(8,128)S(1)} %get-tuple-element.1724), channel_id=1, source_target_pairs={{0,4},{4,8},{8,12},{12,16},{16,20},{20,24},{24,28},{28,32},{32,36}... | collective-permute-start | bytes 196616 | tf_op jit(solution)/shard_map/while/body/eval_jaxpr/ppermute | solution.py:15
  650.0 9.8 %collective-permute-start.7 = (f32[128,128]{1,0:T(8,128)S(1)}, f32[128,128]{1,0:T(8,128)S(1)}, u32[]{:S(2)}, u32[]{:S(2)}) collective-permute-start(f32[128,128]{1,0:T(8,128)S(1)} %get-tuple-element.1725), channel_id=1, source_target_pairs={{0,4},{4,8},{8,12},{12,16},{16,20},{20,24},{24,28},{28,32},{32,36}... | collective-permute-start | bytes 196616 | tf_op jit(solution)/shard_map/while/body/eval_jaxpr/ppermute | solution.py:15
  667.4 8.1 collective-permute-start.6
  670.0 8.0 collective-permute-start.7
  685.3 8.3 collective-permute-start.6
  685.4 8.9 collective-permute-start.7
  700.6 9.8 %collective-permute-start.6 = (f32[128,128]{1,0:T(8,128)S(1)}, f32[128,128]{1,0:T(8,128)S(1)}, u32[]{:S(2)}, u32[]{:S(2)}) collective-permute-start(f32[128,128]{1,0:T(8,128)S(1)} %get-tuple-element.1724), channel_id=1, source_target_pairs={{0,4},{4,8},{8,12},{12,16},{16,20},{20,24},{24,28},{28,32},{32,36}... | collective-permute-start | bytes 196616 | tf_op jit(solution)/shard_map/while/body/eval_jaxpr/ppermute | solution.py:15
  702.3 8.1 collective-permute-start.7
  720.2 8.0 collective-permute-start.6
  720.6 8.2 collective-permute-start.7
  735.9 8.0 collective-permute-start.6
  736.2 8.4 collective-permute-start.7
  752.5 8.8 collective-permute-start.6
  771.2 8.0 collective-permute-start.6
  771.6 8.3 collective-permute-start.7
  786.7 9.7 %collective-permute-start.6 = (f32[128,128]{1,0:T(8,128)S(1)}, f32[128,128]{1,0:T(8,128)S(1)}, u32[]{:S(2)}, u32[]{:S(2)}) collective-permute-start(f32[128,128]{1,0:T(8,128)S(1)} %get-tuple-element.1724), channel_id=1, source_target_pairs={{0,4},{4,8},{8,12},{12,16},{16,20},{20,24},{24,28},{28,32},{32,36}... | collective-permute-start | bytes 196616 | tf_op jit(solution)/shard_map/while/body/eval_jaxpr/ppermute | solution.py:15
  786.8 9.6 %collective-permute-start.7 = (f32[128,128]{1,0:T(8,128)S(1)}, f32[128,128]{1,0:T(8,128)S(1)}, u32[]{:S(2)}, u32[]{:S(2)}) collective-permute-start(f32[128,128]{1,0:T(8,128)S(1)} %get-tuple-element.1725), channel_id=1, source_target_pairs={{0,4},{4,8},{8,12},{12,16},{16,20},{20,24},{24,28},{28,32},{32,36}... | collective-permute-start | bytes 196616 | tf_op jit(solution)/shard_map/while/body/eval_jaxpr/ppermute | solution.py:15
  800.3 10.1 %all-to-all-start.5 = ((bf16[4,32,1024]{2,1,0:T(8,128)(2,1)}), bf16[4,32,1024]{2,1,0:T(8,128)(2,1)S(1)}, u32[]{:S(2)}, u32[]{:S(2)}) async-start(bf16[4,32,1024]{2,1,0:T(8,128)(2,1)} %convert_element_type.193), calls=%async_computation.5 | async-start | bytes 524288 | tf_op jit(solution)/shard_map/all_to_all | solution.py:178
  (82 other events, 3383.0 us)
